TPU v7x, 32 devices: a whole 2x2x4 slice. The times are simulated.
32 devices in a mesh: seq: 2 (over x), ctx: 16 (over z, y, core).
Axes of the slice: x: 2, y: 2, z: 4, core: 2. Of those that a mesh axis runs over, the one named last changes fastest.
Arguments:
- inputs: bfloat16 [2, 2048, 768], P('seq', 'ctx'), may hold values from -6 to 6
- lengths: int32 [2], P('seq'), may hold values from 512 to 2048, as said below
- cotangent: bfloat16 [2, 2048, 768], P('seq', 'ctx'), may hold values from -6 to 6
- w_qkv: bfloat16 [768, 2304], P(('seq', 'ctx')), may hold values from -0.21875 to 0.21875
- w_out: bfloat16 [768, 768], P(('seq', 'ctx')), may hold values from -6 to 6
- w_in: bfloat16 [768, 3072], P(('seq', 'ctx')), may hold values from -0.21875 to 0.21875
- w_back: bfloat16 [3072, 768], P(('seq', 'ctx')), may hold values from -0.109375 to 0.109375
- vectors: bfloat16 [768, 8], P(('seq', 'ctx')), may hold values from -1 to 2
- ffn_bias: bfloat16 [3072], P(('seq', 'ctx')), may hold values from -2 to 2
Outputs:
- result: bfloat16 [2, 2048, 768], P('seq', 'ctx')
- grad_inputs: float32 [2, 2048, 768], P('seq', 'ctx')
- grad_w_qkv: float32 [768, 2304], P(('seq', 'ctx'))
- grad_w_out: float32 [768, 768], P(('seq', 'ctx'))
- grad_w_in: float32 [768, 3072], P(('seq', 'ctx'))
- grad_w_back: float32 [3072, 768], P(('seq', 'ctx'))
- grad_vectors: float32 [768, 8], P(('seq', 'ctx'))
- grad_ffn_bias: float32 [3072], P(('seq', 'ctx'))
Inputs may be any that keep to these rules, and one draw needn't show every extreme that they name: `lengths`: one sequence of each draw is full.
All inputs are finite; a program needn't handle non-finite values.
Results may differ from a plain program's by a relative error of at most 0.025.
Values may be sent and summed in bfloat16 or wider, within the bound.
A program may use at most 448 MiB of HBM per device.

v0:
```python
import jax
import jax.numpy as jnp
from jax import lax
from jax.sharding import PartitionSpec as P

HEADS = 12
EPSILON = 1e-12
MASKED = -1e30


def layer_norm(values_in, norm_gain, norm_shift):
    average = jnp.mean(values_in, axis=-1, keepdims=True)
    centred = values_in - average
    spread = jnp.mean(centred * centred, axis=-1, keepdims=True)
    return centred * lax.rsqrt(spread + EPSILON) * norm_gain + norm_shift


def gelu_exact(values_in):
    return jax.nn.gelu(values_in, approximate=False)


def key_spans(extent_all):
    number_parts = min(8, max(1, -(-extent_all // 2048)))
    span_size = -(-extent_all // number_parts)
    return [
        (offset, min(span_size, extent_all - offset)) for offset in range(0, extent_all, span_size)
    ]


def to_heads(row_block, head_count):
    row_total = row_block.shape[0]
    return row_block.reshape(row_total, head_count, -1).transpose(1, 0, 2)


def online_merge(running, query_heads, key_block, value_block, key_start, length, score_scale):
    top_old, total_old, accum_old = running
    head_count = query_heads.shape[0]
    key_width = key_block.shape[0]
    key_heads = key_block.reshape(key_width, head_count, -1)
    value_heads = value_block.reshape(key_width, head_count, -1)
    scores = (
        jnp.einsum("hqd,khd->hqk", query_heads, key_heads, preferred_element_type=jnp.float32)
        * score_scale
    )
    usable = (key_start + jnp.arange(key_width, dtype=jnp.int32) < length)[None, None, :]
    masked = jnp.where(usable, scores, MASKED)
    top_new = jnp.maximum(top_old, jnp.max(masked, axis=-1))
    factor = jnp.exp(top_old - top_new)
    weights_here = jnp.where(usable, jnp.exp(masked - top_new[:, :, None]), 0.0)
    total_new = total_old * factor + jnp.sum(weights_here, axis=-1)
    accum_new = accum_old * factor[:, :, None] + jnp.einsum(
        "hqk,khd->hqd",
        weights_here.astype(jnp.bfloat16),
        value_heads,
        preferred_element_type=jnp.float32,
    )
    return (top_new, total_new, accum_new)


def score_grads(
    query_heads,
    grad_heads,
    log_total,
    row_delta,
    key_block,
    value_block,
    key_start,
    length,
    score_scale,
):
    head_count = query_heads.shape[0]
    key_width = key_block.shape[0]
    key_heads = key_block.reshape(key_width, head_count, -1)
    value_heads = value_block.reshape(key_width, head_count, -1)
    scores = (
        jnp.einsum("hqd,khd->hqk", query_heads, key_heads, preferred_element_type=jnp.float32)
        * score_scale
    )
    usable = (key_start + jnp.arange(key_width, dtype=jnp.int32) < length)[None, None, :]
    soft_weights = jnp.where(usable, jnp.exp(scores - log_total[:, :, None]), 0.0)
    grad_soft = jnp.einsum(
        "hqd,khd->hqk", grad_heads, value_heads, preferred_element_type=jnp.float32
    )
    grad_scores = (soft_weights * (grad_soft - row_delta[:, :, None])).astype(jnp.bfloat16)
    return (key_heads, grad_scores, soft_weights.astype(jnp.bfloat16))


def per_device(inputs, lengths, cotangent, w_qkv, w_out, w_in, w_back, vectors, ffn_bias):
    own_rows = inputs[0]
    row_count = own_rows.shape[0]
    model_width = own_rows.shape[1]
    head_count = HEADS
    head_size = model_width // head_count
    score_scale = head_size ** (-0.5)
    length = lengths[0]
    ctx_size = lax.axis_size("ctx")
    row_start = lax.axis_index("ctx") * row_count
    qkv_full, vector_full = (
        lax.all_gather(w_qkv, ("seq", "ctx"), axis=0, tiled=True),
        lax.all_gather(vectors, ("seq", "ctx"), axis=0, tiled=True),
    )
    vec = vector_full.astype(jnp.float32)
    projected = jnp.dot(own_rows, qkv_full, preferred_element_type=jnp.float32)
    query_rows = (projected[:, :model_width] + vec[:, 0]).astype(jnp.bfloat16)
    key_rows = projected[:, model_width : 2 * model_width].astype(jnp.bfloat16)
    value_rows = (projected[:, 2 * model_width :] + vec[:, 1]).astype(jnp.bfloat16)
    query_heads = to_heads(query_rows, head_count)
    start_state = (
        jnp.full((head_count, row_count), MASKED, jnp.float32),
        jnp.zeros((head_count, row_count), jnp.float32),
        jnp.zeros((head_count, row_count, head_size), jnp.float32),
    )
    running = start_state
    piece_start = jnp.int32(0)
    key_piece = lax.all_gather(key_rows, "ctx", axis=0, tiled=True)
    value_piece = lax.all_gather(value_rows, "ctx", axis=0, tiled=True)
    for offset, extent in key_spans(key_piece.shape[0]):
        running = online_merge(
            running,
            query_heads,
            key_piece[offset : offset + extent],
            value_piece[offset : offset + extent],
            piece_start + offset,
            length,
            score_scale,
        )
    row_top, row_total, accum = running
    out_full, in_full, back_full, ffn_full = (
        lax.all_gather(w_out, ("seq", "ctx"), axis=0, tiled=True),
        lax.all_gather(w_in, ("seq", "ctx"), axis=0, tiled=True),
        lax.all_gather(w_back, ("seq", "ctx"), axis=0, tiled=True),
        lax.all_gather(ffn_bias, ("seq", "ctx"), axis=0, tiled=True),
    )
    attended_f = accum / row_total[:, :, None]
    log_total = row_top + jnp.log(row_total)
    attended = attended_f.transpose(1, 0, 2).reshape(row_count, model_width).astype(jnp.bfloat16)
    branch = jnp.dot(attended, out_full, preferred_element_type=jnp.float32) + vec[:, 2]
    first_in = own_rows.astype(jnp.float32) + branch
    normed_first, first_back = jax.vjp(layer_norm, first_in, vec[:, 3], vec[:, 4])
    first_low = normed_first.astype(jnp.bfloat16)
    hidden = jnp.dot(first_low, in_full, preferred_element_type=jnp.float32) + ffn_full.astype(
        jnp.float32
    )
    active_f, gelu_back = jax.vjp(gelu_exact, hidden)
    active = active_f.astype(jnp.bfloat16)
    second = jnp.dot(active, back_full, preferred_element_type=jnp.float32) + vec[:, 5]
    result, second_back = jax.vjp(layer_norm, normed_first + second, vec[:, 6], vec[:, 7])
    valid_rows = (row_start + jnp.arange(row_count, dtype=jnp.int32) < length).astype(jnp.float32)[
        :, None
    ]
    grad_result = cotangent[0].astype(jnp.float32) * valid_rows
    grad_second, grad_gain_two, grad_shift_two = second_back(grad_result)
    grad_second_low = grad_second.astype(jnp.bfloat16)
    grad_active = jnp.dot(grad_second_low, back_full.T, preferred_element_type=jnp.float32)
    grad_w_back = jnp.dot(active.T, grad_second_low, preferred_element_type=jnp.float32)
    grad_hidden = gelu_back(grad_active)[0].astype(jnp.bfloat16)
    grad_w_in = jnp.dot(first_low.T, grad_hidden, preferred_element_type=jnp.float32)
    grad_first = grad_second + jnp.dot(grad_hidden, in_full.T, preferred_element_type=jnp.float32)
    grad_branch_full, grad_gain_one, grad_shift_one = first_back(grad_first)
    grad_branch = grad_branch_full.astype(jnp.bfloat16)
    grad_w_out = jnp.dot(attended.T, grad_branch, preferred_element_type=jnp.float32)
    grad_attended = jnp.dot(grad_branch, out_full.T, preferred_element_type=jnp.float32).astype(
        jnp.bfloat16
    )
    grad_heads = to_heads(grad_attended, head_count)
    row_delta = jnp.sum(grad_heads.astype(jnp.float32) * attended_f, axis=-1)
    zero_query = jnp.zeros((head_count, row_count, head_size), jnp.float32)
    key_all, value_all = (
        lax.all_gather(key_rows, "ctx", axis=0, tiled=True),
        lax.all_gather(value_rows, "ctx", axis=0, tiled=True),
    )
    group_size = 1
    while group_size * 2 * row_count <= 2048 and ctx_size % (group_size * 2) == 0:
        group_size = group_size * 2
    block_rows = group_size * row_count
    blocks_total = ctx_size // group_size

    def grad_step(grad_query, block_in):
        key_block, value_block, block_start = block_in
        key_heads, grad_scores, soft_low = score_grads(
            query_heads,
            grad_heads,
            log_total,
            row_delta,
            key_block,
            value_block,
            block_start,
            length,
            score_scale,
        )
        grad_query = (
            grad_query
            + jnp.einsum("hqk,khd->hqd", grad_scores, key_heads, preferred_element_type=jnp.float32)
            * score_scale
        )
        grad_key = (
            jnp.einsum("hqk,hqd->khd", grad_scores, query_heads, preferred_element_type=jnp.float32)
            * score_scale
        )
        grad_value = jnp.einsum(
            "hqk,hqd->khd", soft_low, grad_heads, preferred_element_type=jnp.float32
        )
        joined = jnp.concatenate(
            (
                grad_key.reshape(block_rows, model_width),
                grad_value.reshape(block_rows, model_width),
            ),
            axis=1,
        )
        return (grad_query, joined)

    block_starts = jnp.arange(blocks_total, dtype=jnp.int32) * block_rows
    grad_query, grad_terms = lax.scan(
        grad_step,
        zero_query,
        (
            key_all.reshape(blocks_total, block_rows, model_width),
            value_all.reshape(blocks_total, block_rows, model_width),
            block_starts,
        ),
    )
    owned = lax.psum_scatter(
        grad_terms.reshape(blocks_total * block_rows, 2 * model_width),
        "ctx",
        scatter_dimension=0,
        tiled=True,
    )
    grad_key_rows = owned[:, :model_width]
    grad_value_rows = owned[:, model_width:]
    grad_query_low = (
        grad_query.transpose(1, 0, 2).reshape(row_count, model_width).astype(jnp.bfloat16)
    )
    grad_key_low = grad_key_rows.astype(jnp.bfloat16)
    grad_value_low = grad_value_rows.astype(jnp.bfloat16)
    grad_projected = jnp.concatenate((grad_query_low, grad_key_low, grad_value_low), axis=1)
    grad_w_qkv = jnp.dot(own_rows.T, grad_projected, preferred_element_type=jnp.float32)
    grad_inputs = grad_branch_full + jnp.dot(
        grad_projected, qkv_full.T, preferred_element_type=jnp.float32
    )
    grad_vectors = jnp.stack(
        (
            jnp.sum(grad_query_low.astype(jnp.float32), axis=0),
            jnp.sum(grad_value_low.astype(jnp.float32), axis=0),
            jnp.sum(grad_branch.astype(jnp.float32), axis=0),
            grad_gain_one,
            grad_shift_one,
            jnp.sum(grad_second_low.astype(jnp.float32), axis=0),
            grad_gain_two,
            grad_shift_two,
        ),
        axis=1,
    )
    grad_ffn = jnp.sum(grad_hidden.astype(jnp.float32), axis=0)
    summed_grads = (
        lax.psum_scatter(grad_w_qkv, ("seq", "ctx"), scatter_dimension=0, tiled=True),
        lax.psum_scatter(grad_w_out, ("seq", "ctx"), scatter_dimension=0, tiled=True),
        lax.psum_scatter(grad_w_in, ("seq", "ctx"), scatter_dimension=0, tiled=True),
        lax.psum_scatter(grad_w_back, ("seq", "ctx"), scatter_dimension=0, tiled=True),
        lax.psum_scatter(grad_vectors, ("seq", "ctx"), scatter_dimension=0, tiled=True),
        lax.psum_scatter(grad_ffn, ("seq", "ctx"), scatter_dimension=0, tiled=True),
    )
    return (
        result.astype(jnp.bfloat16)[None],
        grad_inputs[None],
        summed_grads[0],
        summed_grads[1],
        summed_grads[2],
        summed_grads[3],
        summed_grads[4],
        summed_grads[5],
    )


def solution(mesh):
    return jax.shard_map(
        per_device,
        mesh=mesh,
        in_specs=(
            P("seq", "ctx", None),
            P("seq"),
            P("seq", "ctx", None),
            P(("seq", "ctx"), None),
            P(("seq", "ctx"), None),
            P(("seq", "ctx"), None),
            P(("seq", "ctx"), None),
            P(("seq", "ctx"), None),
            P(("seq", "ctx")),
        ),
        out_specs=(
            P("seq", "ctx", None),
            P("seq", "ctx", None),
            P(("seq", "ctx"), None),
            P(("seq", "ctx"), None),
            P(("seq", "ctx"), None),
            P(("seq", "ctx"), None),
            P(("seq", "ctx"), None),
            P(("seq", "ctx")),
        ),
        check_vma=False,
    )
```

profile of v0, /device:TPU:0, one launch (start us, length us, event | category | flops | bytes accessed | tf_op | source)
XLA Modules:
  0.0 1052.9 jit_solution(521782439624674951)
XLA Ops:
  7.9 43.8 %all-gather = bf16[32,24,8]{1,2,0:T(8,128)(2,1)S(1)} all-gather(bf16[1,24,8]{1,2,0:T(8,128)(2,1)} %bitcast.104), channel_id=1, replica_groups=mesh['seq'=2,'ctx'=16] {'seq','ctx'}, dimensions={0}, use_global_device_ids=true | all-gather | bytes 12672 | tf_op jit(solution)/shard_map/all_gather | solution.py:100
  52.1 21.5 %all-gather.8.cloned.1.call-done = bf16[768,2304]{1,0:T(8,128)(2,1)} async-done(((bf16[24,2304]{1,0:T(8,128)(2,1)}), bf16[768,2304]{1,0:T(8,128)(2,1)}) %all-gather.8.cloned.1.call-update) | async-done | bytes 3538960 | tf_op jit(solution)/shard_map/all_gather | solution.py:99
  73.6 2.8 fusion.36
  80.7 39.0 %all-reduce = bf16[3072]{0:T(1024)(128)(2,1)S(1)} all-reduce(bf16[3072]{0:T(1024)(128)(2,1)S(1)} %dynamic-update-slice), channel_id=1, replica_groups=mesh['seq'=2,'ctx'=16] {'seq','ctx'}, use_global_device_ids=true, to_apply=%add | all-reduce | flops 3072 | bytes 12288
  120.4 1.2 all-gather.12.cloned.1.call-done
  121.6 4.7 copy.40
  126.3 42.0 %all-gather.10.cloned.1.call-done = bf16[2048,768]{1,0:T(8,128)(2,1)} async-done(((bf16[128,768]{1,0:T(8,128)(2,1)}), bf16[2048,768]{1,0:T(8,128)(2,1)}) %all-gather.10.cloned.1.call-update) | async-done | bytes 3145744 | tf_op jit(solution)/shard_map/all_gather | solution.py:115
  168.2 4.7 copy.39
  173.0 3.9 select_reduce_fusion
  176.9 3.2 fusion.1
  180.2 1.3 copy-done
  181.4 5.6 fusion.32
  187.0 36.4 %all-gather.14.cloned.1.call-done = bf16[768,768]{1,0:T(8,128)(2,1)} async-done(((bf16[24,768]{1,0:T(8,128)(2,1)}), bf16[768,768]{1,0:T(8,128)(2,1)}) %all-gather.14.cloned.1.call-update) | async-done | bytes 1179664 | tf_op jit(solution)/shard_map/all_gather | solution.py:129
  223.4 1.8 fusion.55
  225.5 63.2 %all-gather.16.cloned.1.call-done = bf16[768,3072]{1,0:T(8,128)(2,1)} async-done(((bf16[24,3072]{1,0:T(8,128)(2,1)}), bf16[768,3072]{1,0:T(8,128)(2,1)}) %all-gather.16.cloned.1.call-update) | async-done | bytes 4718608 | tf_op jit(solution)/shard_map/all_gather | solution.py:130
  288.7 8.4 multiply_convert_fusion.1
  297.1 56.3 %all-gather.18.cloned.1.call-done = bf16[3072,768]{1,0:T(8,128)(2,1)} async-done(((bf16[96,768]{1,0:T(8,128)(2,1)}), bf16[3072,768]{1,0:T(8,128)(2,1)}) %all-gather.18.cloned.1.call-update) | async-done | bytes 4718608 | tf_op jit(solution)/shard_map/all_gather | solution.py:131
  353.4 3.4 fusion.56
  357.3 0.9 fusion.53
  358.9 2.5 convert_reduce_fusion
  361.4 2.4 multiply_reduce_fusion
  366.2 9.9 fusion.3
  376.3 7.3 multiply_convert_fusion
  383.6 4.1 convolution_multiply_fusion
  388.2 11.4 %pad_maximum_fusion = f32[2048,1536]{0,1:T(8,128)} fusion(f32[2048,768]{0,1:T(8,128)} %bitcast.88, f32[2048,768]{0,1:T(8,128)} %bitcast.85), kind=kLoop, calls=%fused_computation | loop fusion | flops 3145728 | bytes 25165824 | tf_op jit(solution)/shard_map/while/body/eval_jaxpr/concatenate | solution.py:203
  399.6 0.9 copy-done.10
  400.5 1.9 fusion.57
  402.7 6.1 fusion.49
  408.9 6.0 fusion.58
  415.0 2.3 copy-done.2
  417.3 6.6 convert_reduce_fusion.4
  423.8 108.9 %reduce-scatter.9.cloned.1.call-done = f32[128,1536]{0,1:T(8,128)} async-done(((f32[2048,1536]{0,1:T(8,128)}), f32[128,1536]{0,1:T(8,128)}) %reduce-scatter.9.cloned.1.call-update) | async-done | bytes 786448 | tf_op jit(solution)/shard_map/reduce_scatter | solution.py:222
  532.8 1.2 convert.9
  534.7 5.0 convolution_bitcast_fusion
  539.6 8.0 copy.43
  548.3 1.0 stack.32
  549.3 1.3 stack.30
  550.6 1.3 stack.31
  551.9 1.3 stack.29
  553.8 1.1 convert_reduce_fusion.3
  554.9 1.4 stack.35
  556.2 40.7 %all-reduce.3 = (f32[768,8]{0,1:T(8,128)}, f32[3072]{0:T(1024)S(1)}) all-reduce(f32[768,8]{0,1:T(8,128)} %stack.35, f32[3072]{0:T(1024)} %get-tuple-element.86), channel_id=7, replica_groups=mesh['seq'=2,'ctx'=16] {'seq','ctx'}, use_global_device_ids=true, to_apply=%region_24.25.clone | all-reduce | flops 9216 | bytes 73728
  597.5 1.4 constant_dynamic-slice_fusion
  598.9 3.3 fusion.19
  602.1 35.7 %reduce-scatter.11.cloned.1.call-done = f32[24,768]{1,0:T(8,128)} async-done(((f32[768,768]{1,0:T(8,128)}), f32[24,768]{1,0:T(8,128)}) %reduce-scatter.11.cloned.1.call-update) | async-done | bytes 73744 | tf_op jit(solution)/shard_map/reduce_scatter | solution.py:256
  637.8 142.0 %reduce-scatter.13.cloned.1.call-done = f32[24,3072]{1,0:T(8,128)} async-done(((f32[768,3072]{1,0:T(8,128)}), f32[24,3072]{1,0:T(8,128)}) %reduce-scatter.13.cloned.1.call-update) | async-done | bytes 294928 | tf_op jit(solution)/shard_map/reduce_scatter | solution.py:257
  779.8 141.8 %reduce-scatter.15.cloned.1.call-done = f32[96,768]{1,0:T(8,128)} async-done(((f32[3072,768]{1,0:T(8,128)}), f32[96,768]{1,0:T(8,128)}) %reduce-scatter.15.cloned.1.call-update) | async-done | bytes 294928 | tf_op jit(solution)/shard_map/reduce_scatter | solution.py:258
  921.6 124.7 %reduce-scatter.17.cloned.1.call-done = f32[24,2304]{1,0:T(8,128)} async-done(((f32[768,2304]{1,0:T(8,128)}), f32[24,2304]{1,0:T(8,128)}) %reduce-scatter.17.cloned.1.call-update) | async-done | bytes 221200
  (100 shorter events, 12.8 us)
Async XLA Ops:
  7.2 66.5 %all-gather.8.cloned.1.call-start = ((), (), s32[]{:S(2)}) async-start(), calls=%async_computation.5 | async-start | bytes 3649536 | tf_op jit(solution)/shard_map/all_gather | solution.py:99
  7.9 113.7 %all-gather.12.cloned.1.call-start = ((), (), s32[]{:S(2)}) async-start(), calls=%async_computation.7 | async-start | bytes 3342336 | tf_op jit(solution)/shard_map/all_gather | solution.py:116
  76.4 4.0 copy-start.14
  77.2 91.1 %all-gather.10.cloned.1.call-start = ((), (), s32[]{:S(2)}) async-start(), calls=%async_computation.6 | async-start | bytes 3342336 | tf_op jit(solution)/shard_map/all_gather | solution.py:115
  77.9 145.5 %all-gather.14.cloned.1.call-start = ((), (), s32[]{:S(2)}) async-start(), calls=%async_computation.8 | async-start | bytes 1216512 | tf_op jit(solution)/shard_map/all_gather | solution.py:129
  78.5 210.2 %all-gather.16.cloned.1.call-start = ((), (), s32[]{:S(2)}) async-start(), calls=%async_computation.9 | async-start | bytes 4866048 | tf_op jit(solution)/shard_map/all_gather | solution.py:130
  79.1 274.3 %all-gather.18.cloned.1.call-start = ((), (), s32[]{:S(2)}) async-start(), calls=%async_computation.10 | async-start | bytes 4866048 | tf_op jit(solution)/shard_map/all_gather | solution.py:131
  79.7 453.1 %reduce-scatter.9.cloned.1.call-start = ((), (), s32[]{:S(2)}) async-start(), calls=%async_computation.11 | async-start | bytes 13369344 | tf_op jit(solution)/shard_map/reduce_scatter | solution.py:222
  176.9 4.6 copy-start
  181.4 42.0 %copy-start.8 = (bf16[1,128,768]{2,1,0:T(8,128)(2,1)S(1)}, bf16[1,128,768]{2,1,0:T(8,128)(2,1)}, u32[]{:S(2)}) copy-start(bf16[1,128,768]{2,1,0:T(8,128)(2,1)} %param.9) | copy-start | bytes 589828
  353.4 5.5 slice-start
  353.4 3.6 copy-start.9
  353.4 3.6 copy-start.12
  353.4 5.5 slice-start.1
  353.4 5.5 copy-start.16
  356.8 2.2 copy-start.15
  358.2 3.2 slice-start.2
  358.9 2.5 slice-start.3
  363.8 1.7 copy-start.5
  364.0 0.8 copy-start.6
  364.1 12.1 %copy-start.13 = (f32[128]{0:T(128)}, f32[128]{0:T(128)S(1)}, u32[]{:S(2)}) copy-start(f32[128]{0:T(128)S(1)} %negate_multiply_fusion.1) | copy-start | bytes 1540
  366.2 9.9 copy-start.11
  366.2 10.0 copy-start.7
  383.6 4.6 copy-start.1
  399.5 0.9 copy-start.10
  399.6 238.3 %reduce-scatter.11.cloned.1.call-start = ((), (), s32[]{:S(2)}) async-start(), calls=%async_computation.12 | async-start | bytes 2433024 | tf_op jit(solution)/shard_map/reduce_scatter | solution.py:256
  402.4 377.4 %reduce-scatter.13.cloned.1.call-start = ((), (), s32[]{:S(2)}) async-start(), calls=%async_computation.13 | async-start | bytes 9732096 | tf_op jit(solution)/shard_map/reduce_scatter | solution.py:257
  408.8 512.8 %reduce-scatter.15.cloned.1.call-start = ((), (), s32[]{:S(2)}) async-start(), calls=%async_computation.14 | async-start | bytes 9732096 | tf_op jit(solution)/shard_map/reduce_scatter | solution.py:258
  414.9 2.4 copy-start.2
  414.9 631.4 %reduce-scatter.17.cloned.1.call-start = ((), (), s32[]{:S(2)}) async-start(), calls=%async_computation.15 | async-start | bytes 7299072
  533.9 0.7 copy-start.4
  547.7 51.2 %copy-start.3 = (bf16[768,2304]{1,0:T(8,128)(2,1)S(1)}, bf16[768,2304]{1,0:T(8,128)(2,1)}, u32[]{:S(2)}) copy-start(bf16[768,2304]{1,0:T(8,128)(2,1)} %all-gather.8.cloned.1.call-done) | copy-start | bytes 10616836
Sparse Core Ops, SparseCore 0:
  10.9 62.7 all-gather.7
  77.3 44.2 all-gather.11
  124.4 43.7 all-gather.9
  171.0 52.3 all-gather.13
  226.2 62.4 all-gather.15
  291.4 61.8 all-gather.17
  399.7 133.0 reduce-scatter.8
  538.6 99.1 reduce-scatter.10
  644.3 135.4 reduce-scatter.12
  786.1 135.4 reduce-scatter.14
  927.9 118.3 reduce-scatter.16
where the time goes:
time: 1050 us
  waiting for transfers between devices  776 us (74%)
  blocking collectives  123 us (12%)
  matrix products  81.4 us (8%)
  local copies, waits for them, and re-layouts  35 us (3%)
  other arithmetic  21.5 us (2%)
  between operations  14.8 us (1%)
    reduce_scatter x1, waiting for transfers between devices, per_device(): lax.psum_scatter(grad_w_in, ('seq', 'ctx'), scatter_dimension=0, tiled=True)  142 us
    reduce_scatter x1, waiting for transfers between devices, per_device(): lax.psum_scatter(grad_w_back, ('seq', 'ctx'), scatter_dimension=0, tiled=...  142 us
    unnamed x12, waiting for transfers between devices  127 us
    reduce_scatter x1, waiting for transfers between devices, per_device(): lax.psum_scatter(grad_terms.reshape(blocks_total * block_rows, 2 * model_...  109 us
    unnamed x2, blocking collectives  79.7 us
    all_gather x1, waiting for transfers between devices, per_device(): lax.all_gather(w_in, ('seq', 'ctx'), axis=0, tiled=True)  63.2 us
    all_gather x1, waiting for transfers between devices, per_device(): lax.all_gather(w_back, ('seq', 'ctx'), axis=0, tiled=True)  56.3 us
    all_gather x1, blocking collectives, per_device(): lax.all_gather(vectors, ('seq', 'ctx'), axis=0, tiled=True)  43.8 us
  transfers between devices with their start and end apart: 11, of which 11 were waited for; matrix products, arithmetic and copies ran while one was open for 8% of the time, Pallas kernels for 0%

commit v1 on v0

--- a/solution.py
+++ b/solution.py
@@ -112,8 +112,12 @@
     )
     running = start_state
     piece_start = jnp.int32(0)
-    key_piece = lax.all_gather(key_rows, "ctx", axis=0, tiled=True)
-    value_piece = lax.all_gather(value_rows, "ctx", axis=0, tiled=True)
+    rows_link = lambda z_in, my_data: jnp.split(
+        lax.all_gather(jnp.concatenate([z_in, my_data], 1), "ctx", axis=0, tiled=True),
+        [z_in.shape[1]],
+        1,
+    )
+    key_piece, value_piece = rows_link(key_rows, value_rows)
     for offset, extent in key_spans(key_piece.shape[0]):
         running = online_merge(
             running,

time: 1050 us -> 1120 us (1.067)
  waiting for transfers between devices: 776 us -> 820 us
  local copies, waits for them, and re-layouts: 35 us -> 46.7 us
    all_gather x2 -> x3, waiting for transfers between devices: 43.2 us -> 93.4 us  [the longest x1 52.9 us: per_device(): lax.all_gather(jnp.concatenate([z_in, my_data], 1), 'ctx', axis=0, tiled=...]
    split x0 -> x3, local copies, waits for them, and re-layouts: none -> 12.5 us  [per_device(): jnp.split(lax.all_gather(jnp.concatenate([z_in, my_data], 1), 'ctx', axis...]
    unnamed x12 -> x13, waiting for transfers between devices: 127 us -> 127 us
  transfers between devices with their start and end apart: 11 -> 12, of which waited for: 11 -> 11; matrix products, arithmetic and copies ran while one was open for 8% -> 9% of each run, Pallas kernels for 0% -> 0%
where the time goes in v1:
time: 1120 us
  waiting for transfers between devices  820 us (73%)
  blocking collectives  123 us (11%)
  matrix products  87 us (8%)
  local copies, waits for them, and re-layouts  46.7 us (4%)
  other arithmetic  25.7 us (2%)
  between operations  15.4 us (1%)
    reduce_scatter x1, waiting for transfers between devices, per_device(): lax.psum_scatter(grad_w_back, ('seq', 'ctx'), scatter_dimension=0, tiled=...  142 us
    reduce_scatter x1, waiting for transfers between devices, per_device(): lax.psum_scatter(grad_w_in, ('seq', 'ctx'), scatter_dimension=0, tiled=True)  142 us
    unnamed x13, waiting for transfers between devices  127 us
    reduce_scatter x1, waiting for transfers between devices, per_device(): lax.psum_scatter(grad_terms.reshape(blocks_total * block_rows, 2 * model_...  109 us
    unnamed x2, blocking collectives  79.7 us
    all_gather x1, waiting for transfers between devices, per_device(): lax.all_gather(w_in, ('seq', 'ctx'), axis=0, tiled=True)  63.2 us
    all_gather x1, waiting for transfers between devices, per_device(): lax.all_gather(w_back, ('seq', 'ctx'), axis=0, tiled=True)  56.4 us
    all_gather x1, waiting for transfers between devices, per_device(): lax.all_gather(jnp.concatenate([z_in, my_data], 1), 'ctx', axis=0, tiled=...  52.9 us
  transfers between devices with their start and end apart: 12, of which 11 were waited for; matrix products, arithmetic and copies ran while one was open for 9% of the time, Pallas kernels for 0%

profile of v1, /device:TPU:0, one launch (start us, length us, event | category | flops | bytes accessed | tf_op | source)
XLA Modules:
  0.0 1118.6 jit_solution(12157068863562952093)
XLA Ops:
  7.9 43.8 %all-gather = bf16[32,24,8]{1,2,0:T(8,128)(2,1)S(1)} all-gather(bf16[1,24,8]{1,2,0:T(8,128)(2,1)} %bitcast.110), channel_id=1, replica_groups=mesh['seq'=2,'ctx'=16] {'seq','ctx'}, dimensions={0}, use_global_device_ids=true | all-gather | bytes 12672 | tf_op jit(solution)/shard_map/all_gather | solution.py:100
  52.7 20.9 %all-gather.9.cloned.1.call-done = bf16[768,2304]{1,0:T(8,128)(2,1)} async-done(((bf16[24,2304]{1,0:T(8,128)(2,1)}), bf16[768,2304]{1,0:T(8,128)(2,1)}) %all-gather.9.cloned.1.call-update) | async-done | bytes 3538960 | tf_op jit(solution)/shard_map/all_gather | solution.py:99
  73.6 2.8 fusion.37
  78.0 1.8 pad_maximum_fusion.2
  82.7 39.1 %all-reduce = bf16[3072]{0:T(1024)(128)(2,1)S(1)} all-reduce(bf16[3072]{0:T(1024)(128)(2,1)S(1)} %dynamic-update-slice), channel_id=1, replica_groups=mesh['seq'=2,'ctx'=16] {'seq','ctx'}, use_global_device_ids=true, to_apply=%add | all-reduce | flops 3072 | bytes 12288
  123.1 4.7 copy.48
  127.8 40.5 %all-gather.19.cloned.1.call-done = bf16[2048,768]{1,0:T(8,128)(2,1)} async-done(((bf16[128,768]{1,0:T(8,128)(2,1)}), bf16[2048,768]{1,0:T(8,128)(2,1)}) %all-gather.19.cloned.1.call-update) | async-done | bytes 3145744 | tf_op jit(solution)/shard_map/all_gather | solution.py:173
  168.3 3.2 copy.46
  171.5 6.4 fusion.59
  177.9 52.9 %all-gather.11.cloned.1.call-done = bf16[2048,1536]{1,0:T(8,128)(2,1)} async-done(((bf16[128,1536]{1,0:T(8,128)(2,1)}), bf16[2048,1536]{1,0:T(8,128)(2,1)}) %all-gather.11.cloned.1.call-update) | async-done | bytes 6291472 | tf_op jit(solution)/shard_map/all_gather | solution.py:116
  230.8 4.9 fusion.56
  235.7 4.7 copy.44
  240.4 2.9 copy.45
  243.3 3.8 fusion
  247.2 3.2 fusion.2
  251.1 5.6 fusion.33
  256.7 29.5 %all-gather.13.cloned.1.call-done = bf16[768,768]{1,0:T(8,128)(2,1)} async-done(((bf16[24,768]{1,0:T(8,128)(2,1)}), bf16[768,768]{1,0:T(8,128)(2,1)}) %all-gather.13.cloned.1.call-update) | async-done | bytes 1179664 | tf_op jit(solution)/shard_map/all_gather | solution.py:133
  286.2 1.8 fusion.57
  288.3 63.2 %all-gather.15.cloned.1.call-done = bf16[768,3072]{1,0:T(8,128)(2,1)} async-done(((bf16[24,3072]{1,0:T(8,128)(2,1)}), bf16[768,3072]{1,0:T(8,128)(2,1)}) %all-gather.15.cloned.1.call-update) | async-done | bytes 4718608 | tf_op jit(solution)/shard_map/all_gather | solution.py:134
  351.5 8.4 multiply_convert_fusion.1
  359.9 56.4 %all-gather.17.cloned.1.call-done = bf16[3072,768]{1,0:T(8,128)(2,1)} async-done(((bf16[96,768]{1,0:T(8,128)(2,1)}), bf16[3072,768]{1,0:T(8,128)(2,1)}) %all-gather.17.cloned.1.call-update) | async-done | bytes 4718608 | tf_op jit(solution)/shard_map/all_gather | solution.py:135
  416.4 3.4 fusion.58
  422.5 2.4 convert_reduce_fusion
  425.0 2.4 multiply_reduce_fusion
  429.0 1.2 convolution_convert_fusion
  431.4 9.9 fusion.4
  441.5 7.5 multiply_convert_fusion
  449.0 4.1 convolution_multiply_fusion
  453.6 11.4 %pad_maximum_fusion = f32[2048,1536]{0,1:T(8,128)} fusion(f32[2048,768]{0,1:T(8,128)} %bitcast.92, f32[2048,768]{0,1:T(8,128)} %bitcast.91), kind=kLoop, calls=%fused_computation | loop fusion | flops 3145728 | bytes 25165824 | tf_op jit(solution)/shard_map/while/body/eval_jaxpr/concatenate | solution.py:207
  465.9 1.9 fusion.60
  467.9 6.0 fusion.50
  474.9 6.0 fusion.61
  481.0 2.3 copy-done.1
  483.3 6.0 convert_reduce_fusion.4
  489.3 109.0 %reduce-scatter.9.cloned.1.call-done = f32[128,1536]{0,1:T(8,128)} async-done(((f32[2048,1536]{0,1:T(8,128)}), f32[128,1536]{0,1:T(8,128)}) %reduce-scatter.9.cloned.1.call-update) | async-done | bytes 786448 | tf_op jit(solution)/shard_map/reduce_scatter | solution.py:226
  600.2 4.0 convolution_bitcast_fusion
  604.2 8.0 copy.50
  614.2 1.3 stack.30
  615.4 1.3 stack.31
  616.7 1.3 stack.29
  619.7 1.3 stack.35
  621.1 40.6 %all-reduce.3 = (f32[768,8]{0,1:T(8,128)}, f32[3072]{0:T(1024)S(1)}) all-reduce(f32[768,8]{0,1:T(8,128)} %stack.35, f32[3072]{0:T(1024)} %get-tuple-element.86), channel_id=7, replica_groups=mesh['seq'=2,'ctx'=16] {'seq','ctx'}, use_global_device_ids=true, to_apply=%region_24.25.clone | all-reduce | flops 9216 | bytes 73728
  662.3 1.4 constant_dynamic-slice_fusion
  663.6 3.3 fusion.20
  666.9 36.5 %reduce-scatter.11.cloned.1.call-done = f32[24,768]{1,0:T(8,128)} async-done(((f32[768,768]{1,0:T(8,128)}), f32[24,768]{1,0:T(8,128)}) %reduce-scatter.11.cloned.1.call-update) | async-done | bytes 73744 | tf_op jit(solution)/shard_map/reduce_scatter | solution.py:260
  703.4 141.8 %reduce-scatter.13.cloned.1.call-done = f32[24,3072]{1,0:T(8,128)} async-done(((f32[768,3072]{1,0:T(8,128)}), f32[24,3072]{1,0:T(8,128)}) %reduce-scatter.13.cloned.1.call-update) | async-done | bytes 294928 | tf_op jit(solution)/shard_map/reduce_scatter | solution.py:261
  845.2 141.9 %reduce-scatter.15.cloned.1.call-done = f32[96,768]{1,0:T(8,128)} async-done(((f32[3072,768]{1,0:T(8,128)}), f32[96,768]{1,0:T(8,128)}) %reduce-scatter.15.cloned.1.call-update) | async-done | bytes 294928 | tf_op jit(solution)/shard_map/reduce_scatter | solution.py:262
  987.1 124.7 %reduce-scatter.17.cloned.1.call-done = f32[24,2304]{1,0:T(8,128)} async-done(((f32[768,2304]{1,0:T(8,128)}), f32[24,2304]{1,0:T(8,128)}) %reduce-scatter.17.cloned.1.call-update) | async-done | bytes 221200
  (154 shorter events, 21.8 us)
Async XLA Ops:
  7.2 66.5 %all-gather.9.cloned.1.call-start = ((), (), s32[]{:S(2)}) async-start(), calls=%async_computation.5 | async-start | bytes 3649536 | tf_op jit(solution)/shard_map/all_gather | solution.py:99
  7.9 115.2 %all-gather.21.cloned.1.call-start = ((), (), s32[]{:S(2)}) async-start(), calls=%async_computation.11 | async-start | bytes 3342336 | tf_op jit(solution)/shard_map/all_gather | solution.py:174
  76.4 6.0 copy-start.37
  77.2 91.1 %all-gather.19.cloned.1.call-start = ((), (), s32[]{:S(2)}) async-start(), calls=%async_computation.10 | async-start | bytes 3342336 | tf_op jit(solution)/shard_map/all_gather | solution.py:173
  77.9 152.8 %all-gather.11.cloned.1.call-start = ((), (), s32[]{:S(2)}) async-start(), calls=%async_computation.6 | async-start | bytes 6684672 | tf_op jit(solution)/shard_map/all_gather | solution.py:116
  79.8 206.4 %all-gather.13.cloned.1.call-start = ((), (), s32[]{:S(2)}) async-start(), calls=%async_computation.7 | async-start | bytes 1216512 | tf_op jit(solution)/shard_map/all_gather | solution.py:133
  80.4 271.1 %all-gather.15.cloned.1.call-start = ((), (), s32[]{:S(2)}) async-start(), calls=%async_computation.8 | async-start | bytes 4866048 | tf_op jit(solution)/shard_map/all_gather | solution.py:134
  81.0 335.4 %all-gather.17.cloned.1.call-start = ((), (), s32[]{:S(2)}) async-start(), calls=%async_computation.9 | async-start | bytes 4866048 | tf_op jit(solution)/shard_map/all_gather | solution.py:135
  81.7 516.5 %reduce-scatter.9.cloned.1.call-start = ((), (), s32[]{:S(2)}) async-start(), calls=%async_computation.12 | async-start | bytes 13369344 | tf_op jit(solution)/shard_map/reduce_scatter | solution.py:226
  122.9 128.2 %copy-start.20 = (pred[2048]{0:T(1024)(128)(4,1)}, pred[2048]{0:T(1024)(128)(4,1)S(1)}, u32[]{:S(2)}) copy-start(pred[2048]{0:T(1024)(128)(4,1)S(1)} %iota_compare_fusion) | copy-start | bytes 6148
  171.5 6.4 copy-start
  251.1 35.2 %copy-start.10 = (bf16[1,128,768]{2,1,0:T(8,128)(2,1)S(1)}, bf16[1,128,768]{2,1,0:T(8,128)(2,1)}, u32[]{:S(2)}) copy-start(bf16[1,128,768]{2,1,0:T(8,128)(2,1)} %param.9) | copy-start | bytes 589828
  251.1 35.2 %copy-start.26 = (f32[768]{0:T(1024)S(1)}, f32[768]{0:T(1024)}, u32[]{:S(2)}) copy-start(f32[768]{0:T(1024)} %get-tuple-element.81) | copy-start | bytes 9220
  256.7 94.8 %copy-start.32 = (f32[3072]{0:T(1024)S(1)}, f32[3072]{0:T(1024)}, u32[]{:S(2)}) copy-start(f32[3072]{0:T(1024)} %convert_element_type.108) | copy-start | bytes 36868
  288.1 136.9 %copy-start.22 = (f32[128]{0:T(128)}, f32[128]{0:T(128)S(1)}, u32[]{:S(2)}) copy-start(f32[128]{0:T(128)S(1)} %broadcast_multiply_fusion.1) | copy-start | bytes 1540
  288.3 71.6 %copy-start.35 = (f32[128]{0:T(128)}, f32[128]{0:T(128)S(1)}, u32[]{:S(2)}) copy-start(f32[128]{0:T(128)S(1)} %multiply_reduce_fusion.4) | copy-start | bytes 1540
  288.3 128.0 %copy-start.29 = (f32[128]{0:T(128)}, f32[128]{0:T(128)S(1)}, u32[]{:S(2)}) copy-start(f32[128]{0:T(128)S(1)} %fusion.39) | copy-start | bytes 1540
  351.5 64.8 %copy-start.25 = (f32[768]{0:T(1024)S(1)}, f32[768]{0:T(1024)}, u32[]{:S(2)}) copy-start(f32[768]{0:T(1024)} %get-tuple-element.78) | copy-start | bytes 9220
  416.3 6.1 slice-start
  416.3 3.6 copy-start.12
  416.4 3.6 copy-start.33
  416.4 4.5 copy-start.24
  416.4 6.1 slice-start.1
  416.4 6.1 copy-start.39
  419.8 2.7 copy-start.38
  421.8 3.2 slice-start.2
  422.5 2.5 copy-start.14
  422.5 2.5 slice-start.3
  422.5 2.5 copy-start.30
  425.0 2.4 copy-start.8
  425.0 4.0 copy-start.5
  427.4 4.0 copy-start.17
  428.3 13.0 %copy-start.6 = (f32[128,768]{1,0:T(8,128)}, f32[128,768]{1,0:T(8,128)S(1)}, u32[]{:S(2)}) copy-start(f32[128,768]{1,0:T(8,128)S(1)} %get-tuple-element.93) | copy-start | bytes 1179652
  431.4 10.0 copy-start.16
  431.4 10.0 copy-start.18
  431.4 10.0 copy-start.19
  431.4 10.1 copy-start.7
  431.4 10.1 copy-start.21
  449.0 4.6 copy-start.2
  465.0 2.9 copy-start.9
  465.0 2.9 copy-start.23
  465.0 2.9 copy-start.31
  465.0 238.3 %reduce-scatter.11.cloned.1.call-start = ((), (), s32[]{:S(2)}) async-start(), calls=%async_computation.13 | async-start | bytes 2433024 | tf_op jit(solution)/shard_map/reduce_scatter | solution.py:260
  467.8 377.4 %reduce-scatter.13.cloned.1.call-start = ((), (), s32[]{:S(2)}) async-start(), calls=%async_computation.14 | async-start | bytes 9732096 | tf_op jit(solution)/shard_map/reduce_scatter | solution.py:261
  474.0 513.1 %reduce-scatter.15.cloned.1.call-start = ((), (), s32[]{:S(2)}) async-start(), calls=%async_computation.15 | async-start | bytes 9732096 | tf_op jit(solution)/shard_map/reduce_scatter | solution.py:262
  480.9 630.8 %reduce-scatter.17.cloned.1.call-start = ((), (), s32[]{:S(2)}) async-start(), calls=%async_computation.16 | async-start | bytes 7299072
  489.3 114.9 %copy-start.11 = (bf16[12,128,64]{1,2,0:T(8,128)(2,1)}, bf16[12,128,64]{1,2,0:T(8,128)(2,1)S(1)}, u32[]{:S(2)}) copy-start(bf16[12,128,64]{1,2,0:T(8,128)(2,1)S(1)} %get-tuple-element.120) | copy-start | bytes 589828
  612.2 51.4 %copy-start.3 = (bf16[768,2304]{1,0:T(8,128)(2,1)S(1)}, bf16[768,2304]{1,0:T(8,128)(2,1)}, u32[]{:S(2)}) copy-start(bf16[768,2304]{1,0:T(8,128)(2,1)} %all-gather.9.cloned.1.call-done) | copy-start | bytes 10616836
  (8 other events, 10.1 us)
Sparse Core Ops, SparseCore 0:
  10.9 62.7 all-gather.8
  77.3 44.2 all-gather.20
  124.5 43.7 all-gather.18
  171.0 59.7 all-gather.10
  233.5 52.6 all-gather.12
  289.0 62.4 all-gather.14
  354.4 61.8 all-gather.16
  465.1 133.0 reduce-scatter.8
  604.1 99.2 reduce-scatter.10
  709.7 135.4 reduce-scatter.12
  851.7 135.3 reduce-scatter.14
  993.2 118.5 reduce-scatter.16
